TPU v7x, 32 devices: a whole 2x2x4 slice. The times are simulated.
32 devices in a mesh: slab: 2 (over x), line: 8 (over z, y), band: 2 (over core).
Axes of the slice: x: 2, y: 2, z: 4, core: 2. Of those that a mesh axis runs over, the one named last changes fastest.
Arguments:
- cube: bfloat16 [230, 2048, 256], P('band', ('slab', 'line')), parts along dimension 1, may hold values from -6 to 6
- observed: bfloat16 [13, 2048, 256], P(None, ('slab', 'line')), parts along dimension 1, may hold values from -6 to 6
- along_kernels: bfloat16 [3, 128, 128], replicated, may hold values from -0.3125 to 0.3125
- along_offsets: int32 [3], replicated, may hold values from -1 to 1, as said below
- across_kernels: bfloat16 [3, 128, 128], replicated, may hold values from -0.3125 to 0.3125
- across_offsets: int32 [3], replicated, may hold values from -1 to 1, as said below
- resp_start: int32 [13], replicated, may hold values from 0 to 21
- resp_values: bfloat16 [13, 20], replicated, may hold values from 0.049804688 to 0.3984375
Outputs:
- synthetic: float32 [13, 2048, 256], P(None, ('slab', 'line')), parts along dimension 1
- angles: float32 [2048, 256], P(('slab', 'line')), parts along dimension 0
There are 2 independent parts, one for each index of `slab`. A program takes and returns all parts, laid end to end along the dimension named above; an argument that names none is the same for every part. Nothing has to cross between parts.
Inputs may be any that keep to these rules, and one draw needn't show every extreme that they name: `along_offsets`: the three entries are -1, 0 and 1, each once. `across_offsets`: the three entries are -1, 0 and 1, each once.
All inputs are finite; a program needn't handle non-finite values.
Results may differ from a plain program's by a relative error of at most 0.0003.
Values may be sent and summed in bfloat16 or wider, within the bound.
A program may use at most 192 MiB of HBM per device.

v0:
```python
import jax
import jax.numpy as jnp
from jax import lax
from jax.sharding import PartitionSpec as P

BLK = 128
SPB = 10


def extended(shard, sides, width):
    for axis, dim in sides:
        size, length = (lax.axis_size(axis), shard.shape[dim])
        up = [(i, (i + 1) % size) for i in range(size - 1)]
        down = [(j, i) for i, j in up]
        last = lax.slice_in_dim(shard, length - width, length, axis=dim)
        leading = lax.slice_in_dim(shard, 0, width, axis=dim)
        before = lax.ppermute(last, axis, up)
        after = lax.ppermute(leading, axis, down)
        shard = jnp.concatenate([before, shard, after], axis=dim)
    return shard


def pick_kernels(kernels, offsets):
    shifts = jnp.arange(3, dtype=jnp.int32) - 1
    onehot = (offsets[None, :] == shifts[:, None]).astype(jnp.float32)
    return jnp.einsum(
        "sk,kpq->spq", onehot, kernels.astype(jnp.float32), precision=lax.Precision.HIGHEST
    )


def dense_response(resp_start, resp_values, band_total):
    bands = jnp.arange(band_total, dtype=jnp.int32)
    local = bands[None, :] - SPB * resp_start[:, None]
    slots = jnp.arange(2 * SPB, dtype=jnp.int32)
    hits = local[:, :, None] == slots[None, None, :]
    return jnp.sum(
        jnp.where(hits, resp_values.astype(jnp.float32)[:, None, :], jnp.float32(0.0)), axis=-1
    )


def along_blocks(padded, chosen, count):
    total = None
    for index in range(3):
        term = jnp.einsum(
            "pq,bnqc->bnpc",
            chosen[index],
            padded[:, index : index + count],
            precision=lax.Precision.HIGHEST,
        )
        total = term if total is None else total + term
    return total


def across_filter(field, chosen):
    count = field.shape[2] // BLK
    blocks = field.reshape(field.shape[0], field.shape[1], count, BLK)
    padded = jnp.pad(blocks, ((0, 0), (0, 0), (1, 1), (0, 0)))
    total = jnp.zeros(blocks.shape, jnp.float32)
    for index in range(3):
        total = total + jnp.einsum(
            "pq,blnq->blnp",
            chosen[index],
            padded[:, :, index : index + count],
            precision=lax.Precision.HIGHEST,
        )
    return total.reshape(field.shape)


def respond_plain(weights, field):
    return jnp.einsum(
        "mb,blc->mlc", weights.astype(jnp.bfloat16), field, preferred_element_type=jnp.float32
    )


def on_device(
    cube,
    observed,
    along_kernels,
    along_offsets,
    across_kernels,
    across_offsets,
    resp_start,
    resp_values,
):
    band_share = cube.shape[0]
    line_rows = cube.shape[1]
    column_count = cube.shape[2]
    band_total = band_share * lax.axis_size("band")
    along_pick = pick_kernels(along_kernels, along_offsets)
    across_pick = pick_kernels(across_kernels, across_offsets)
    response = dense_response(resp_start, resp_values, band_total)
    local_response = lax.dynamic_slice_in_dim(
        response, lax.axis_index("band") * band_share, band_share, 1
    )
    count = line_rows // BLK
    folded = respond_plain(local_response, cube)
    summed = lax.psum(folded, "band")
    padded_sum = extended(summed, (("line", 1),), BLK)
    padded = padded_sum.reshape(summed.shape[0], count + 2, BLK, column_count)
    smooth = along_blocks(padded, along_pick, count).reshape(summed.shape)
    partial_value = across_filter(smooth, across_pick)
    seen = observed.astype(jnp.float32)
    inner = jnp.sum(partial_value * seen, axis=0)
    first = jnp.sqrt(jnp.sum(partial_value * partial_value, axis=0))
    second = jnp.sqrt(jnp.sum(seen * seen, axis=0))
    angles = jnp.arccos(jnp.clip(inner / jnp.maximum(first * second, 1.0), -1.0, 1.0))
    return (partial_value, angles)


def solution(mesh):
    placed = (
        P("band", ("slab", "line"), None),
        P(None, ("slab", "line"), None),
        P(),
        P(),
        P(),
        P(),
        P(),
        P(),
    )
    return jax.shard_map(
        on_device,
        mesh=mesh,
        in_specs=placed,
        out_specs=(P(None, ("slab", "line"), None), P(("slab", "line"), None)),
        check_vma=False,
    )
```

profile of v0, /device:TPU:5, one launch (start us, length us, event | category | flops | bytes accessed | tf_op | source)
XLA Modules:
  0.0 156.4 jit_solution(8674825454620172075)
XLA Ops:
  7.2 0.7 broadcast_multiply_fusion
  8.0 0.7 convert_element_type.8
  8.7 0.1 select_reduce_fusion
  8.8 8.8 %fusion = f32[13,128,256]{2,0,1:T(8,128)} fusion(bf16[115,128,256]{2,1,0:T(8,128)(2,1)} %param.8, bf16[13,230]{1,0:T(8,128)(2,1)S(1)} %select_reduce_fusion, s32[]{:T(128)S(6)} %select_n.8), kind=kOutput, calls=%fused_computation | convolution fusion | flops 97976320 | bytes 9244676 | tf_op jit(solution)/shard_map/mb,blc->mlc/dot_general | solution.py:70
  17.6 23.3 %all-reduce.3.cloned.1.call-done = f32[13,128,256]{2,0,1:T(8,128)} async-done(((f32[13,128,256]{2,0,1:T(8,128)}), f32[13,128,256]{2,0,1:T(8,128)}) %all-reduce.3.cloned.1.call-update) | async-done | bytes 1703952 | tf_op jit(solution)/shard_map/psum | solution.py:97
  41.0 2.6 %copy.36 = f32[13,128,256]{2,1,0:T(8,128)S(1)} copy(f32[13,128,256]{2,0,1:T(8,128)} %all-reduce.3.cloned.1.call-done) | data formatting | bytes 3407872 | tf_op jit(solution)/shard_map/psum | solution.py:97
  43.6 3.1 %collective-permute-start = (f32[13,128,256]{2,1,0:T(8,128)S(1)}, f32[13,128,256]{2,1,0:T(8,128)S(1)}, u32[]{:S(2)}, u32[]{:S(2)}) collective-permute-start(f32[13,128,256]{2,1,0:T(8,128)S(1)} %copy.36), channel_id=1, source_target_pairs={{0,2},{2,4},{4,6},{6,8},{8,10},{10,12},{12,14},{1,3},{3,5},{5,7},{... | collective-permute-start | bytes 5111816 | tf_op jit(solution)/shard_map/ppermute | solution.py:17
  46.7 2.3 %collective-permute-start.1 = (f32[13,128,256]{2,1,0:T(8,128)S(1)}, f32[13,128,256]{2,1,0:T(8,128)S(1)}, u32[]{:S(2)}, u32[]{:S(2)}) collective-permute-start(f32[13,128,256]{2,1,0:T(8,128)S(1)} %copy.36), channel_id=1, source_target_pairs={{2,0},{4,2},{6,4},{8,6},{10,8},{12,10},{14,12},{3,1},{5,3},{7,5},{... | collective-permute-start | bytes 5111816 | tf_op jit(solution)/shard_map/ppermute | solution.py:18
  49.0 0.3 fusion.14
  49.3 0.3 fusion.12
  49.6 0.1 fusion.29
  49.7 0.8 fusion.28
  50.5 70.0 %collective-permute-done = f32[13,128,256]{2,1,0:T(8,128)S(1)} collective-permute-done((f32[13,128,256]{2,1,0:T(8,128)S(1)}, f32[13,128,256]{2,1,0:T(8,128)S(1)}, u32[]{:S(2)}, u32[]{:S(2)}) %collective-permute-start) | collective-permute-done | bytes 1703968 | tf_op jit(solution)/shard_map/ppermute | solution.py:17
  120.5 1.0 copy.38
  121.5 1.0 copy.39
  122.6 0.6 copy-done.1
  123.1 0.7 pad_maximum_fusion
  123.9 2.6 %fusion.27 = (f32[13,1,128,256]{3,0,2,1:T(8,128)S(1)}, f32[13,1,128,256]{3,0,2,1:T(8,128)}, f32[13,1,128,256]{3,0,2,1:T(8,128)}) fusion(f32[13,3,128,256]{3,0,2,1:T(8,128)S(1)} %bitcast.67), kind=kLoop, calls=%fused_computation.37 | loop fusion | bytes 10223616 | tf_op jit(solution)/shard_map/slice | solution.py:47
  126.5 2.9 %copy.55 = f32[13,1,128,256]{2,3,0,1:T(8,128)} copy(f32[13,1,128,256]{3,0,2,1:T(8,128)} %get-tuple-element.11) | data formatting | bytes 3407872
  129.4 2.8 %copy.56 = f32[13,1,128,256]{2,3,0,1:T(8,128)} copy(f32[13,1,128,256]{3,0,2,1:T(8,128)} %get-tuple-element.12) | data formatting | bytes 3407872
  132.2 1.8 %copy.54 = f32[13,1,128,256]{2,3,0,1:T(8,128)} copy(f32[13,1,128,256]{3,0,2,1:T(8,128)S(1)} %get-tuple-element.10) | data formatting | bytes 3407872
  133.9 3.1 %fusion.6 = f32[13,256,128]{2,1,0:T(8,128)S(1)} fusion(f32[128,128,1]{1,0,2:T(8,128)S(1)} %bitcast.75, f32[13,1,128,256]{2,3,0,1:T(8,128)} %copy.55), kind=kOutput, calls=%fused_computation.9 | convolution fusion | flops 654311424 | bytes 3473408 | tf_op jit(solution)/shard_map/pq,bnqc->bnpc/dot_general | solution.py:44
  137.1 1.6 %fusion.4 = f32[13,256,128]{2,1,0:T(8,128)S(1)} fusion(f32[128,128,1]{1,0,2:T(8,128)S(1)} %bitcast.74, f32[13,1,128,256]{2,3,0,1:T(8,128)S(1)} %copy-done.3), kind=kOutput, calls=%fused_computation.7 | convolution fusion | flops 654311424 | bytes 3473408 | tf_op jit(solution)/shard_map/pq,bnqc->bnpc/dot_general | solution.py:44
  138.7 1.6 %add_add_fusion.1 = f32[13,256,128]{2,1,0:T(8,128)S(1)} fusion(f32[13,256,128]{2,1,0:T(8,128)S(1)} %fusion.4, f32[13,256,128]{2,1,0:T(8,128)S(1)} %fusion.6, f32[128,128,1]{1,0,2:T(8,128)S(1)} %bitcast.71, f32[13,1,128,256]{2,3,0,1:T(8,128)S(1)} %copy-done.4), kind=kOutput, calls=%fused_computation.15 | convolution fusion | flops 655163392 | bytes 6881280 | tf_op jit(solution)/shard_map/pq,bnqc->bnpc/dot_general | solution.py:44
  140.3 1.6 %fusion.30 = f32[13,128,2,128]{1,3,2,0:T(8,128)S(1)} fusion(f32[13,128,2,128]{1,3,2,0:T(8,128)S(1)} %bitcast.64, f32[128,128,1,1]{1,0,3,2:T(8,128)S(1)} %bitcast.73), kind=kOutput, calls=%fused_computation.40 | convolution fusion | flops 654311424 | bytes 3473408 | tf_op jit(solution)/shard_map/pq,blnq->blnp/dot_general | solution.py:60
  141.9 1.5 fusion.31
  143.4 1.8 %multiply_reduce_fusion = (f32[128,2,128]{0,2,1:T(8,128)}, f32[13,128,2,128]{1,3,2,0:T(8,128)S(1)}) fusion(f32[13,128,2,128]{1,3,2,0:T(8,128)S(1)} %bitcast.66, f32[128,128,1,1]{1,0,3,2:T(8,128)S(1)} %bitcast.70, f32[13,128,2,128]{1,3,2,0:T(8,128)S(1)} %fusion.31, f32[13,128,2,128]{1,3,2,0:T(8,128)S(1)} %fusion.30), kind=kOutput, calls=%fused_computation.13 | convolution fusion | flops 328826880 | bytes 7012352 | tf_op jit(solution)/shard_map/pq,blnq->blnp/dot_general | solution.py:60
  145.2 0.7 copy.49
  146.0 1.1 sqrt.9
  147.1 0.1 copy.48
  147.2 1.5 fusion.3
  148.6 1.0 sqrt_atan2_fusion
  (22 shorter events, 0.2 us)
Async XLA Ops:
  7.2 41.8 %copy-start = (bf16[3,128,128]{2,1,0:T(8,128)(2,1)S(1)}, bf16[3,128,128]{2,1,0:T(8,128)(2,1)}, u32[]{:S(2)}) copy-start(bf16[3,128,128]{2,1,0:T(8,128)(2,1)} %param.10) | copy-start | bytes 294916
  7.2 33.8 %all-reduce.3.cloned.1.call-start = ((), (), s32[]{:S(2)}) async-start(), calls=%async_computation | async-start | bytes 4194304 | tf_op jit(solution)/shard_map/psum | solution.py:97
  17.6 31.4 %copy-start.7 = (s32[3]{0:T(128)S(1)}, s32[3]{0:T(128)}, u32[]{:S(2)}) copy-start(s32[3]{0:T(128)} %param.11) | copy-start | bytes 40
  17.6 31.7 %copy-start.6 = (bf16[3,128,128]{2,1,0:T(8,128)(2,1)S(1)}, bf16[3,128,128]{2,1,0:T(8,128)(2,1)}, u32[]{:S(2)}) copy-start(bf16[3,128,128]{2,1,0:T(8,128)(2,1)} %param.12) | copy-start | bytes 294916
  17.6 31.6 %copy-start.8 = (s32[3]{0:T(128)S(1)}, s32[3]{0:T(128)}, u32[]{:S(2)}) copy-start(s32[3]{0:T(128)} %param.13) | copy-start | bytes 40
  43.6 76.9 %collective-permute-start = (f32[13,128,256]{2,1,0:T(8,128)S(1)}, f32[13,128,256]{2,1,0:T(8,128)S(1)}, u32[]{:S(2)}, u32[]{:S(2)}) collective-permute-start(f32[13,128,256]{2,1,0:T(8,128)S(1)} %copy.36), channel_id=1, source_target_pairs={{0,2},{2,4},{4,6},{6,8},{8,10},{10,12},{12,14},{1,3},{3,5},{5,7},{... | collective-permute-start | bytes 5111816 | tf_op jit(solution)/shard_map/ppermute | solution.py:17
  46.7 74.9 %collective-permute-start.1 = (f32[13,128,256]{2,1,0:T(8,128)S(1)}, f32[13,128,256]{2,1,0:T(8,128)S(1)}, u32[]{:S(2)}, u32[]{:S(2)}) collective-permute-start(f32[13,128,256]{2,1,0:T(8,128)S(1)} %copy.36), channel_id=1, source_target_pairs={{2,0},{4,2},{6,4},{8,6},{10,8},{12,10},{14,12},{3,1},{5,3},{7,5},{... | collective-permute-start | bytes 5111816 | tf_op jit(solution)/shard_map/ppermute | solution.py:18
  121.5 1.6 %copy-start.1 = (f32[13,128,256]{2,0,1:T(8,128)S(1)}, f32[13,128,256]{2,0,1:T(8,128)}, u32[]{:S(2)}) copy-start(f32[13,128,256]{2,0,1:T(8,128)} %all-reduce.3.cloned.1.call-done) | copy-start | bytes 5111812
  133.9 3.1 %copy-start.3 = (f32[13,1,128,256]{2,3,0,1:T(8,128)S(1)}, f32[13,1,128,256]{2,3,0,1:T(8,128)}, u32[]{:S(2)}) copy-start(f32[13,1,128,256]{2,3,0,1:T(8,128)} %copy.56) | copy-start | bytes 5111812
  137.1 1.6 %copy-start.4 = (f32[13,1,128,256]{2,3,0,1:T(8,128)S(1)}, f32[13,1,128,256]{2,3,0,1:T(8,128)}, u32[]{:S(2)}) copy-start(f32[13,1,128,256]{2,3,0,1:T(8,128)} %copy.54) | copy-start | bytes 5111812
  141.9 1.5 copy-start.5
  146.0 3.6 %copy-start.2 = (f32[13,128,256]{2,1,0:T(8,128)}, f32[13,128,256]{2,1,0:T(8,128)S(1)}, u32[]{:S(2)}) copy-start(f32[13,128,256]{2,1,0:T(8,128)S(1)} %copy.49) | copy-start | bytes 5111812
Sparse Core Ops, SparseCore 0:
  17.7 23.2 all-reduce.2
where the time goes:
time: 158 us; the launch traced here: 156 us
  waiting for transfers between devices  93.4 us (59%)
  matrix products  20.5 us (13%)
  local copies, waits for them, and re-layouts  18.1 us (11%)
  between operations  14.3 us (9%)
  starting transfers between devices  5.42 us (3%)
  other arithmetic  4.75 us (3%)
    ppermute x1, waiting for transfers between devices, extended(): before = lax.ppermute(last, axis, up)  70 us
    psum x1, waiting for transfers between devices, on_device(): summed = lax.psum(folded, 'band')  23.3 us
    dot_general x1, matrix products, respond_plain(): jnp.einsum('mb,blc->mlc', weights.astype(jnp.bfloat16), field, preferred_...  8.77 us
    unnamed x22, local copies, waits for them, and re-layouts  8.75 us
    dot_general x3, matrix products, along_blocks(): jnp.einsum('pq,bnqc->bnpc', chosen[index], padded[:, index:index + count]...  6.31 us
    dot_general x3, matrix products, across_filter(): jnp.einsum('pq,blnq->blnp', chosen[index], padded[:, :, index:index + cou...  4.89 us
  transfers between devices with their start and end apart: 3, of which 2 were waited for; matrix products, arithmetic and copies ran while one was open for 2% of the time, Pallas kernels for 0%

commit v1 on v0

v1 whole, which is shorter than its diff:
```python
import functools

import jax
import jax.numpy as jnp
from jax import lax
from jax.experimental import pallas as pl
from jax.experimental.pallas import tpu as pltpu
from jax.sharding import PartitionSpec as P

BLK = 128
SPB = 10
ROWS = 16
LAG = 2
MESH = pl.DeviceIdType.MESH
F32 = jnp.float32
BF16 = jnp.bfloat16


def halves(value):
    high = value.astype(BF16)
    low = (value - high.astype(F32)).astype(BF16)
    return high, low


def picked(kernels, offsets, shift):
    total = None
    for k in range(3):
        term = jnp.where(offsets[k] == shift, kernels[k].astype(F32), 0.0)
        total = term if total is None else total + term
    return total


def iota(shape, dim):
    return lax.broadcasted_iota(jnp.int32, shape, dim)


def kernel(
    sizes,
    cube,
    observed,
    along_hbm,
    across_hbm,
    values,
    along_off,
    across_off,
    start,
    synthetic,
    cosine,
    folder,
    field,
    seen,
    along,
    across,
    taps,
    mixer,
    given,
    own,
    got,
    total,
    coded,
    scale,
    near,
    near_scale,
    far,
    far_scale,
    result,
    angle_buf,
    cube_sem,
    arg_sem,
    give_sem,
    got_sem,
    send_sem,
    near_sem,
    scale_send_sem,
    near_scale_sem,
    pass_sem,
    far_sem,
    scale_pass_sem,
    far_scale_sem,
    share_sem,
    result_sem,
    out_sem,
):
    bands, lines, columns, ms, half, line_size = sizes
    groups = lines // ROWS
    core = lax.axis_index("band")
    index = lax.axis_index("line")
    other = {"band": 1 - core}
    even = index % 2 == 0
    partner = {"line": index + 1 - 2 * (index % 2)}
    step = 2 - 4 * (index % 2)
    ahead, behind = index + step, index - step
    has_ahead = jnp.logical_and(ahead >= 0, ahead < line_size)
    has_behind = jnp.logical_and(behind >= 0, behind < line_size)

    def cube_copy(g):
        return pltpu.make_async_copy(
            cube.at[:, pl.ds(g * ROWS, ROWS), :], field.at[g], cube_sem.at[g]
        )

    along_copy = pltpu.make_async_copy(along_hbm, along, arg_sem.at[0])
    across_copy = pltpu.make_async_copy(across_hbm, across, arg_sem.at[1])
    seen_copy = pltpu.make_async_copy(observed, seen, arg_sem.at[2])
    for g in range(groups):
        cube_copy(g).start()
    along_copy.start()
    across_copy.start()
    seen_copy.start()

    barrier = pltpu.get_barrier_semaphore()
    pl.semaphore_signal(barrier, inc=1, device_id=other, device_id_type=MESH)
    pl.semaphore_signal(barrier, inc=1, device_id=partner, device_id_type=MESH)

    @pl.when(has_ahead)
    def _():
        pl.semaphore_signal(barrier, inc=1, device_id={"line": ahead}, device_id_type=MESH)

    @pl.when(has_behind)
    def _():
        pl.semaphore_signal(barrier, inc=1, device_id={"line": behind}, device_id_type=MESH)

    lane = core * bands + iota((ms, 128), 1)
    row = iota((ms, 128), 0)
    first = jnp.zeros((ms, 128), jnp.int32)
    for m in range(ms):
        first = jnp.where(row == m, start[m], first)
    slot = lane - SPB * first
    weights = values[...].astype(F32)
    response = jnp.zeros((ms, 128), F32)
    for j in range(2 * SPB):
        response = jnp.where(slot == j, weights[:, j : j + 1], response)
    tall = 2 * half * ROWS
    picks = iota((tall, ms), 0) // ROWS
    owner = jnp.where(picks < half, (1 - core) * half + picks, core * half + picks - half)
    choose = (owner == iota((tall, ms), 1)).astype(BF16)
    per_row = jnp.dot(choose, response.astype(BF16), preferred_element_type=F32).astype(BF16)
    wide = bands * ROWS
    spread = (iota((128, wide), 1) // ROWS == iota((128, wide), 0)).astype(BF16)
    spread_rows = jnp.dot(per_row, spread, preferred_element_type=F32)
    same = iota((tall, wide), 0) % ROWS == iota((tall, wide), 1) % ROWS
    folder[...] = jnp.where(same, spread_rows, 0.0).astype(BF16)

    peers = 2 + has_ahead.astype(jnp.int32) + has_behind.astype(jnp.int32)
    pl.semaphore_wait(barrier, peers)

    def give_copy(g):
        return pltpu.make_async_remote_copy(
            src_ref=given.at[g],
            dst_ref=got.at[g],
            send_sem=give_sem.at[g],
            recv_sem=got_sem.at[g],
            device_id=other,
            device_id_type=MESH,
        )

    def fold(g, carry):
        cube_copy(g).wait()
        block = field[g].reshape(wide, columns)
        part = jnp.dot(folder[...], block, preferred_element_type=F32)
        part = part.reshape(2 * half, ROWS, columns)
        given[g] = part[:half]
        own[g] = part[half:]
        give_copy(g).start()
        return carry

    lax.fori_loop(0, groups, fold, 0)

    along_copy.wait()
    across_copy.wait()
    before, after = (picked(along, along_off, -1), picked(along, along_off, 1))
    middle = picked(along, along_off, 0)
    near_tap = jnp.where(even, after, before)
    far_tap = jnp.where(even, before, after)
    for slot_index, tap in enumerate((middle, near_tap, far_tap)):
        tap = tap.astype(BF16)
        taps[slot_index] = jnp.concatenate([tap, tap], axis=1)
    count = columns // BLK
    mixer[...] = jnp.zeros(mixer.shape, BF16)
    for shift in (-1, 0, 1):
        turned = jnp.transpose(picked(across, across_off, shift)).astype(BF16)
        for j in range(count):
            if 0 <= j + shift < count:
                for part in range(2):
                    top = part * columns + (j + shift) * BLK
                    mixer[top : top + BLK, j * BLK : (j + 1) * BLK] = turned

    def code_copies(m):
        return (
            pltpu.make_async_remote_copy(
                src_ref=coded.at[m],
                dst_ref=near.at[m],
                send_sem=send_sem.at[m],
                recv_sem=near_sem.at[m],
                device_id=partner,
                device_id_type=MESH,
            ),
            pltpu.make_async_remote_copy(
                src_ref=scale.at[m],
                dst_ref=near_scale.at[m],
                send_sem=scale_send_sem.at[m],
                recv_sem=near_scale_sem.at[m],
                device_id=partner,
                device_id_type=MESH,
            ),
        )

    def pass_copies(m):
        return (
            pltpu.make_async_remote_copy(
                src_ref=near.at[m],
                dst_ref=far.at[m],
                send_sem=pass_sem.at[m],
                recv_sem=far_sem.at[m],
                device_id={"line": ahead},
                device_id_type=MESH,
            ),
            pltpu.make_async_remote_copy(
                src_ref=near_scale.at[m],
                dst_ref=far_scale.at[m],
                send_sem=scale_pass_sem.at[m],
                recv_sem=far_scale_sem.at[m],
                device_id={"line": ahead},
                device_id_type=MESH,
            ),
        )

    def share_copy(m):
        return pltpu.make_async_remote_copy(
            src_ref=result.at[0, m],
            dst_ref=result.at[1, m],
            send_sem=share_sem.at[m],
            recv_sem=result_sem.at[m],
            device_id=other,
            device_id_type=MESH,
        )

    def out_copy(which, m):
        place = core if which == 0 else 1 - core
        return pltpu.make_async_copy(
            result.at[which, m], synthetic.at[place * half + m], out_sem.at[which, m]
        )

    def guard(m, place, body):
        if half + m < ms:
            body()
        else:
            pl.when(place * half + m < ms)(body)

    @pl.when(jnp.logical_not(has_behind))
    def _():
        far[...] = jnp.zeros(far.shape, jnp.int16)
        far_scale[...] = jnp.zeros(far_scale.shape, F32)

    for g in range(groups):
        give_copy(g).wait_recv()

    for m in range(half):

        def encode(m=m):
            value = (own[:, m] + got[:, m]).reshape(lines, columns)
            total[m] = value
            peak = jnp.max(jnp.abs(value), axis=0, keepdims=True)
            inverse = jnp.where(peak > 0.0, 32767.0 / jnp.maximum(peak, 1e-30), 0.0)
            coded[m] = jnp.round(value * inverse).astype(jnp.int32).astype(jnp.int16)
            scale[m] = peak * (1.0 / 32767.0)
            for copy in code_copies(m):
                copy.start()

        guard(m, core, encode)

    seen_copy.wait()

    def filtered(slot_index, value):
        high, low = halves(value)
        stacked = jnp.concatenate([high, low], axis=0)
        return jnp.dot(taps[slot_index], stacked, preferred_element_type=F32)

    def arrive(m):
        copies = code_copies(m)
        for copy in copies:
            copy.wait_recv()

        @pl.when(has_ahead)
        def _():
            for copy in pass_copies(m):
                copy.start()

        total[m] = (
            filtered(0, total[m])
            + filtered(1, near[m].astype(jnp.int32).astype(F32)) * near_scale[m]
        )

    def finish(m):
        @pl.when(has_behind)
        def _():
            for copy in pass_copies(m):
                copy.wait_recv()

        smooth = total[m] + filtered(2, far[m].astype(jnp.int32).astype(F32)) * far_scale[m]
        high, low = halves(smooth)
        both = jnp.concatenate([high, low], axis=1)
        result[0, m] = jnp.dot(both, mixer[...], preferred_element_type=F32)
        share_copy(m).start()
        out_copy(0, m).start()

    for tick in range(half + LAG):
        if tick < half:
            guard(tick, core, functools.partial(arrive, tick))
        if tick >= LAG:
            guard(tick - LAG, core, functools.partial(finish, tick - LAG))

    for m in range(half):

        def receive(m=m):
            share_copy(m).wait_recv()
            out_copy(1, m).start()

        guard(m, 1 - core, receive)

    def angle(r, carry):
        rows = pl.ds(r * ROWS, ROWS)
        inner = power = level = None
        for which in range(2):
            place = core if which == 0 else 1 - core
            sums = [jnp.zeros((ROWS, columns), F32)] * 3
            for m in range(half):
                spot = place * half + m
                valid = spot < ms
                look = jnp.minimum(spot, ms - 1)
                mine = result[which, m, rows, :]
                sight = seen[look, rows, :].astype(F32)
                if half + m >= ms:
                    mine = jnp.where(valid, mine, 0.0)
                    sight = jnp.where(valid, sight, 0.0)
                sums = [
                    sums[0] + mine * sight,
                    sums[1] + mine * mine,
                    sums[2] + sight * sight,
                ]
            inner = sums[0] if inner is None else inner + sums[0]
            power = sums[1] if power is None else power + sums[1]
            level = sums[2] if level is None else level + sums[2]
        norm = jnp.maximum(jnp.sqrt(power) * jnp.sqrt(level), 1.0)
        angle_buf[rows, :] = jnp.clip(inner / norm, -1.0, 1.0)
        return carry

    def blank(which, place):
        for m in range(half):
            if half + m >= ms:

                @pl.when(place * half + m >= ms)
                def _():
                    result[which, m] = jnp.zeros((lines, columns), F32)

    blank(0, core)
    blank(1, 1 - core)
    lax.fori_loop(0, lines // ROWS, angle, 0)
    cos_copy = pltpu.make_async_copy(angle_buf, cosine, arg_sem.at[3])
    cos_copy.start()

    for g in range(groups):
        give_copy(g).wait_send()
    for m in range(half):

        def drain(m=m):
            for copy in code_copies(m):
                copy.wait_send()

            @pl.when(has_ahead)
            def _():
                for copy in pass_copies(m):
                    copy.wait_send()

            share_copy(m).wait_send()
            out_copy(0, m).wait()

        guard(m, core, drain)
        guard(m, 1 - core, lambda m=m: out_copy(1, m).wait())
    cos_copy.wait()


def on_device(
    cube,
    observed,
    along_kernels,
    along_offsets,
    across_kernels,
    across_offsets,
    resp_start,
    resp_values,
):
    bands, lines, columns = cube.shape
    ms = observed.shape[0]
    cores = lax.axis_size("band")
    line_size = lax.axis_size("line")
    assert cores == 2 and line_size % 2 == 0 and lines == BLK and bands <= 128
    half = -(-ms // cores)
    groups = lines // ROWS
    sizes = (bands, lines, columns, ms, half, line_size)
    hbm = pl.BlockSpec(memory_space=pltpu.HBM)
    vmem = pl.BlockSpec(memory_space=pltpu.VMEM)
    smem = pl.BlockSpec(memory_space=pltpu.SMEM)
    dma = pltpu.SemaphoreType.DMA
    synthetic, cosine = pl.pallas_call(
        functools.partial(kernel, sizes),
        out_shape=(
            jax.ShapeDtypeStruct((ms, lines, columns), F32),
            jax.ShapeDtypeStruct((lines, columns), F32),
        ),
        in_specs=[hbm, hbm, hbm, hbm, vmem, smem, smem, smem],
        out_specs=(hbm, hbm),
        scratch_shapes=[
            pltpu.VMEM((2 * half * ROWS, bands * ROWS), BF16),
            pltpu.VMEM((groups, bands, ROWS, columns), BF16),
            pltpu.VMEM((ms, lines, columns), BF16),
            pltpu.VMEM((3, BLK, BLK), BF16),
            pltpu.VMEM((3, BLK, BLK), BF16),
            pltpu.VMEM((3, BLK, 2 * BLK), BF16),
            pltpu.VMEM((2 * columns, columns), BF16),
            pltpu.VMEM((groups, half, ROWS, columns), F32),
            pltpu.VMEM((groups, half, ROWS, columns), F32),
            pltpu.VMEM((groups, half, ROWS, columns), F32),
            pltpu.VMEM((half, lines, columns), F32),
            pltpu.VMEM((half, lines, columns), jnp.int16),
            pltpu.VMEM((half, 1, columns), F32),
            pltpu.VMEM((half, lines, columns), jnp.int16),
            pltpu.VMEM((half, 1, columns), F32),
            pltpu.VMEM((half, lines, columns), jnp.int16),
            pltpu.VMEM((half, 1, columns), F32),
            pltpu.VMEM((2, half, lines, columns), F32),
            pltpu.VMEM((lines, columns), F32),
            dma((groups,)),
            dma((4,)),
            dma((groups,)),
            dma((groups,)),
        ]
        + [dma((half,))] * 10
        + [dma((2, half))],
        compiler_params=pltpu.CompilerParams(
            collective_id=0, has_side_effects=True, vmem_limit_bytes=48 * 2**20
        ),
    )(
        cube,
        observed,
        along_kernels,
        across_kernels,
        resp_values,
        along_offsets,
        across_offsets,
        resp_start,
    )
    return synthetic, jnp.arccos(cosine)


def solution(mesh):
    placed = (
        P("band", ("slab", "line"), None),
        P(None, ("slab", "line"), None),
        P(),
        P(),
        P(),
        P(),
        P(),
        P(),
    )
    return jax.shard_map(
        on_device,
        mesh=mesh,
        in_specs=placed,
        out_specs=(P(None, ("slab", "line"), None), P(("slab", "line"), None)),
        check_vma=False,
    )
```

time: 158 us -> 35.3 us (0.22)
  waiting for transfers between devices: 93.4 us -> 0 us
  Pallas kernels: 0 us -> 26.6 us
  matrix products: 20.5 us -> 0 us
  between operations: 14.3 us -> 0.66 us
  local copies, waits for them, and re-layouts: 18.1 us -> 6.77 us
  starting transfers between devices: 5.42 us -> 0 us
  other arithmetic: 4.75 us -> 0.91 us
    ppermute x2 -> x0, waiting for transfers between devices: 70 us -> none  [the longest x1 70 us: extended(): before = lax.ppermute(last, axis, up)]
    pallas_call x0 -> x1, Pallas kernels: none -> 26.6 us  [on_device(): pl.pallas_call(functools.partial(kernel, sizes), out_shape=(jax.ShapeDtyp...]
    psum x1 -> x0, waiting for transfers between devices: 23.3 us -> none  [on_device(): summed = lax.psum(folded, 'band')]
    dot_general x9 -> x0, matrix products: 20.5 us -> none  [the longest x1 8.77 us: respond_plain(): jnp.einsum('mb,blc->mlc', weights.astype(jnp.bfloat16), field, preferred_...]
    ppermute x2 -> x0, starting transfers between devices: 5.39 us -> none  [the longest x1 3.1 us: extended(): before = lax.ppermute(last, axis, up)]
    slice x3 -> x0, local copies, waits for them, and re-layouts: 3.55 us -> none  [the longest x1 2.65 us: along_blocks(): padded[:, index:index + count]]
    psum x1 -> x0, local copies, waits for them, and re-layouts: 2.58 us -> none  [on_device(): summed = lax.psum(folded, 'band')]
    ppermute x2 -> x0, local copies, waits for them, and re-layouts: 2.03 us -> none  [the longest x1 1.01 us: extended(): after = lax.ppermute(leading, axis, down)]
  transfers between devices with their start and end apart: 3 -> 0, of which waited for: 2 -> 0; matrix products, arithmetic and copies ran while one was open for 2% -> 0% of each run, Pallas kernels for 0% -> 0%
where the time goes in v1:
time: 35.3 us; the launch traced here: 35 us
  Pallas kernels  26.6 us (75%)
  local copies, waits for them, and re-layouts  6.77 us (19%)
  other arithmetic  0.91 us (3%)
  between operations  0.66 us (2%)
    pallas_call x1, Pallas kernels, on_device(): pl.pallas_call(functools.partial(kernel, sizes), out_shape=(jax.ShapeDtyp...  26.6 us
    unnamed x15, local copies, waits for them, and re-layouts  6.77 us
    another operation x1, other arithmetic, on_device(): return (synthetic, jnp.arccos(cosine))  0.91 us

profile of v1, /device:TPU:5, one launch (start us, length us, event | category | flops | bytes accessed | tf_op | source)
XLA Modules:
  0.0 35.0 jit_solution(8359520751007954612)
XLA Ops:
  0.6 0.0 copy-start
  0.6 1.1 %copy-done = bf16[13,128,256]{2,1,0:T(8,128)(2,1)S(1)} copy-done((bf16[13,128,256]{2,1,0:T(8,128)(2,1)S(1)}, bf16[13,128,256]{2,1,0:T(8,128)(2,1)}, u32[]{:S(2)}) %copy-start) | copy-done | bytes 851992
  1.8 0.0 copy-start.1
  1.8 0.9 %copy-done.1 = bf16[3,128,128]{2,1,0:T(8,128)(2,1)S(1)} copy-done((bf16[3,128,128]{2,1,0:T(8,128)(2,1)S(1)}, bf16[3,128,128]{2,1,0:T(8,128)(2,1)}, u32[]{:S(2)}) %copy-start.1) | copy-done | bytes 98328
  2.7 0.0 copy-start.2
  2.7 0.9 %copy-done.2 = bf16[3,128,128]{2,1,0:T(8,128)(2,1)S(1)} copy-done((bf16[3,128,128]{2,1,0:T(8,128)(2,1)S(1)}, bf16[3,128,128]{2,1,0:T(8,128)(2,1)}, u32[]{:S(2)}) %copy-start.2) | copy-done | bytes 98328
  3.6 0.0 copy-start.3
  3.6 0.7 %copy-done.3 = bf16[13,20]{1,0:T(8,128)(2,1)S(1)} copy-done((bf16[13,20]{1,0:T(8,128)(2,1)S(1)}, bf16[13,20]{1,0:T(8,128)(2,1)}, u32[]{:S(2)}) %copy-start.3) | copy-done | bytes 544
  4.3 0.0 copy-start.4
  4.3 0.7 %copy-done.4 = s32[3]{0:T(128)S(1)} copy-done((s32[3]{0:T(128)S(1)}, s32[3]{0:T(128)}, u32[]{:S(2)}) %copy-start.4) | copy-done | bytes 36
  4.9 0.0 copy-start.5
  4.9 0.7 %copy-done.5 = s32[3]{0:T(128)S(1)} copy-done((s32[3]{0:T(128)S(1)}, s32[3]{0:T(128)}, u32[]{:S(2)}) %copy-start.5) | copy-done | bytes 36
  5.6 0.0 copy-start.6
  5.6 0.7 %copy-done.6 = s32[13]{0:T(128)S(1)} copy-done((s32[13]{0:T(128)S(1)}, s32[13]{0:T(128)}, u32[]{:S(2)}) %copy-start.6) | copy-done | bytes 76
  6.2 26.6 %shard_map.95 = (f32[13,128,256]{2,1,0:T(8,128)S(1)}, f32[128,256]{1,0:T(8,128)S(1)}) custom-call(bf16[115,128,256]{2,1,0:T(8,128)(2,1)} %cube.1, bf16[13,128,256]{2,1,0:T(8,128)(2,1)S(1)} %copy-done, bf16[3,128,128]{2,1,0:T(8,128)(2,1)S(1)} %copy-done.1, bf16[3,128,128]{2,1,0:T(8,128)(2,1)S(1)} %copy-done.2, bf16[13,20]{1,0:T(8,128)(2,1)S(1)} %copy-done.3, ...), custom_call_target="tpu_custom_call" | custom-call | tf_op jit(solution)/shard_map/pallas_call | solution.py:404
  32.9 0.9 %sqrt_atan2_fusion = f32[128,256]{1,0:T(8,128)} fusion(f32[128,256]{1,0:T(8,128)S(1)} %get-tuple-element.5), kind=kLoop, calls=%fused_computation | loop fusion | flops 98304 | bytes 262144 | tf_op jit(solution)/shard_map/acos | solution.py:452
  33.8 1.2 %copy.11 = f32[13,128,256]{2,1,0:T(8,128)} copy(f32[13,128,256]{2,1,0:T(8,128)S(1)} %get-tuple-element.8) | data formatting | bytes 3407872
Async XLA Ops:
  0.6 1.2 %copy-start = (bf16[13,128,256]{2,1,0:T(8,128)(2,1)S(1)}, bf16[13,128,256]{2,1,0:T(8,128)(2,1)}, u32[]{:S(2)}) copy-start(bf16[13,128,256]{2,1,0:T(8,128)(2,1)} %observed.1) | copy-start | bytes 2555908
  1.8 0.9 %copy-start.1 = (bf16[3,128,128]{2,1,0:T(8,128)(2,1)S(1)}, bf16[3,128,128]{2,1,0:T(8,128)(2,1)}, u32[]{:S(2)}) copy-start(bf16[3,128,128]{2,1,0:T(8,128)(2,1)} %along_hbm.1) | copy-start | bytes 294916
  2.7 0.9 %copy-start.2 = (bf16[3,128,128]{2,1,0:T(8,128)(2,1)S(1)}, bf16[3,128,128]{2,1,0:T(8,128)(2,1)}, u32[]{:S(2)}) copy-start(bf16[3,128,128]{2,1,0:T(8,128)(2,1)} %across_hbm.1) | copy-start | bytes 294916
  3.6 0.7 %copy-start.3 = (bf16[13,20]{1,0:T(8,128)(2,1)S(1)}, bf16[13,20]{1,0:T(8,128)(2,1)}, u32[]{:S(2)}) copy-start(bf16[13,20]{1,0:T(8,128)(2,1)} %values.1) | copy-start | bytes 1564
  4.3 0.7 %copy-start.4 = (s32[3]{0:T(128)S(1)}, s32[3]{0:T(128)}, u32[]{:S(2)}) copy-start(s32[3]{0:T(128)} %along_off.1) | copy-start | bytes 40
  4.9 0.7 %copy-start.5 = (s32[3]{0:T(128)S(1)}, s32[3]{0:T(128)}, u32[]{:S(2)}) copy-start(s32[3]{0:T(128)} %across_off.1) | copy-start | bytes 40
  5.6 0.7 %copy-start.6 = (s32[13]{0:T(128)S(1)}, s32[13]{0:T(128)}, u32[]{:S(2)}) copy-start(s32[13]{0:T(128)} %start.1) | copy-start | bytes 160

commit v2 on v1

--- a/solution.py
+++ b/solution.py
@@ -40,10 +40,10 @@
     observed,
     along_hbm,
     across_hbm,
-    values,
-    along_off,
-    across_off,
-    start,
+    values_hbm,
+    along_off_hbm,
+    across_off_hbm,
+    start_hbm,
     synthetic,
     cosine,
     folder,
@@ -65,6 +65,10 @@
     far_scale,
     result,
     angle_buf,
+    values,
+    along_off,
+    across_off,
+    start,
     cube_sem,
     arg_sem,
     give_sem,
@@ -101,6 +105,14 @@
     along_copy = pltpu.make_async_copy(along_hbm, along, arg_sem.at[0])
     across_copy = pltpu.make_async_copy(across_hbm, across, arg_sem.at[1])
     seen_copy = pltpu.make_async_copy(observed, seen, arg_sem.at[2])
+    early = [
+        pltpu.make_async_copy(values_hbm, values, arg_sem.at[4]),
+        pltpu.make_async_copy(start_hbm, start, arg_sem.at[5]),
+        pltpu.make_async_copy(along_off_hbm, along_off, arg_sem.at[6]),
+        pltpu.make_async_copy(across_off_hbm, across_off, arg_sem.at[7]),
+    ]
+    for copy in early:
+        copy.start()
     for g in range(groups):
         cube_copy(g).start()
     along_copy.start()
@@ -118,6 +130,9 @@
     @pl.when(has_behind)
     def _():
         pl.semaphore_signal(barrier, inc=1, device_id={"line": behind}, device_id_type=MESH)
+
+    for copy in early:
+        copy.wait()
 
     lane = core * bands + iota((ms, 128), 1)
     row = iota((ms, 128), 0)
@@ -398,8 +413,6 @@
     groups = lines // ROWS
     sizes = (bands, lines, columns, ms, half, line_size)
     hbm = pl.BlockSpec(memory_space=pltpu.HBM)
-    vmem = pl.BlockSpec(memory_space=pltpu.VMEM)
-    smem = pl.BlockSpec(memory_space=pltpu.SMEM)
     dma = pltpu.SemaphoreType.DMA
     synthetic, cosine = pl.pallas_call(
         functools.partial(kernel, sizes),
@@ -407,7 +420,7 @@
             jax.ShapeDtypeStruct((ms, lines, columns), F32),
             jax.ShapeDtypeStruct((lines, columns), F32),
         ),
-        in_specs=[hbm, hbm, hbm, hbm, vmem, smem, smem, smem],
+        in_specs=[hbm] * 8,
         out_specs=(hbm, hbm),
         scratch_shapes=[
             pltpu.VMEM((2 * half * ROWS, bands * ROWS), BF16),
@@ -429,15 +442,19 @@
             pltpu.VMEM((half, 1, columns), F32),
             pltpu.VMEM((2, half, lines, columns), F32),
             pltpu.VMEM((lines, columns), F32),
+            pltpu.VMEM(resp_values.shape, BF16),
+            pltpu.SMEM(along_offsets.shape, jnp.int32),
+            pltpu.SMEM(across_offsets.shape, jnp.int32),
+            pltpu.SMEM(resp_start.shape, jnp.int32),
             dma((groups,)),
-            dma((4,)),
+            dma((8,)),
             dma((groups,)),
             dma((groups,)),
         ]
         + [dma((half,))] * 10
         + [dma((2, half))],
         compiler_params=pltpu.CompilerParams(
-            collective_id=0, has_side_effects=True, vmem_limit_bytes=48 * 2**20
+            collective_id=0, has_side_effects=True, vmem_limit_bytes=67_043_328
         ),
     )(
         cube,

time: 35.3 us -> 31.2 us (0.88)
  local copies, waits for them, and re-layouts: 6.77 us -> 2.75 us
  other arithmetic: 0.91 us -> 1.81 us
  Pallas kernels: 26.6 us -> 25.8 us
    unnamed x15 -> x1, local copies, waits for them, and re-layouts: 6.77 us -> 2.75 us
    another operation x1, other arithmetic: 0.91 us -> 1.81 us  [on_device(): return (synthetic, jnp.arccos(cosine))]
    pallas_call x1, Pallas kernels: 26.6 us -> 25.8 us  [on_device(): pl.pallas_call(functools.partial(kernel, sizes), out_shape=(jax.ShapeDtyp...]
where the time goes in v2:
time: 31.2 us; the launch traced here: 31 us
  Pallas kernels  25.8 us (83%)
  local copies, waits for them, and re-layouts  2.75 us (9%)
  other arithmetic  1.81 us (6%)
  between operations  0.64 us (2%)
    pallas_call x1, Pallas kernels, on_device(): pl.pallas_call(functools.partial(kernel, sizes), out_shape=(jax.ShapeDtyp...  25.8 us
    unnamed x1, local copies, waits for them, and re-layouts  2.75 us
    another operation x1, other arithmetic, on_device(): return (synthetic, jnp.arccos(cosine))  1.81 us

profile of v2, /device:TPU:5, one launch (start us, length us, event | category | flops | bytes accessed | tf_op | source)
XLA Modules:
  0.0 31.0 jit_solution(5194363175250048302)
XLA Ops:
  0.6 25.8 %shard_map.95 = (f32[13,128,256]{2,1,0:T(8,128)}, f32[128,256]{1,0:T(8,128)}) custom-call(bf16[115,128,256]{2,1,0:T(8,128)(2,1)} %cube.1, bf16[13,128,256]{2,1,0:T(8,128)(2,1)} %observed.1, bf16[3,128,128]{2,1,0:T(8,128)(2,1)} %along_hbm.1, bf16[3,128,128]{2,1,0:T(8,128)(2,1)} %across_hbm.1, bf16[13,20]{1,0:T(8,128)(2,1)} %values_hbm.1, s32[3]{0:T(128)} %along_off_hbm.1, ...), custom_call_target="tpu_custom_call" | custom-call | tf_op jit(solution)/shard_map/pallas_call | solution.py:417
  26.5 1.8 %sqrt_atan2_fusion = f32[128,256]{1,0:T(8,128)} fusion(f32[128,256]{1,0:T(8,128)} %get-tuple-element.5), kind=kLoop, calls=%fused_computation | loop fusion | flops 98304 | bytes 262144 | tf_op jit(solution)/shard_map/acos | solution.py:469
  28.3 2.8 %copy.11 = f32[13,128,256]{2,1,0:T(8,128)} copy(f32[13,128,256]{2,1,0:T(8,128)} %get-tuple-element.8) | data formatting | bytes 3407872
